TPU v7x, 32 devices: a whole 2x2x4 slice. The times are simulated.
32 devices in a mesh: seq: 16 (over z, y, core), blk: 2 (over x).
Axes of the slice: x: 2, y: 2, z: 4, core: 2. Of those that a mesh axis runs over, the one named last changes fastest.
Arguments:
- tokens: bfloat16 [32, 1024, 512], P('seq', 'blk'), may hold values from -6 to 6
- memory: bfloat16 [32, 512, 512], P('seq', 'blk'), may hold values from -6 to 6
- segment_ends: int32 [32, 1024], P('seq', 'blk'), may hold values from 1 to 8192, as said below
- memory_ends: int32 [32, 512], P('seq', 'blk'), may hold values from -4088 to 0, as said below
- segment_counts: int32 [32], P('seq'), may hold values from 512 to 1024, as said below
- memory_lengths: int32 [32], P('seq'), may hold values from 128 to 512, as said below
- first_gain: float32 [512], replicated, may hold values from 0.5 to 1.5
- first_shift: float32 [512], replicated, may hold values from -1.2 to 1.2
- query_weight: bfloat16 [512, 512], replicated, may hold values from -0.25 to 0.25
- key_weight: bfloat16 [512, 512], replicated, may hold values from -0.25 to 0.25
- value_weight: bfloat16 [512, 512], replicated, may hold values from -0.25 to 0.25
- out_weight: bfloat16 [512, 512], replicated, may hold values from -2 to 2
- head_slopes: float32 [8], replicated, may hold values from 1e-05 to 0.03
- second_gain: float32 [512], replicated, may hold values from 0.5 to 1.5
- second_shift: float32 [512], replicated, may hold values from -1.2 to 1.2
- hidden_weight: bfloat16 [512, 2048], replicated, may hold values from -0.25 to 0.25
- output_weight: bfloat16 [2048, 512], replicated, may hold values from -0.125 to 0.125
- output_grad: bfloat16 [32, 1024, 512], P('seq', 'blk'), may hold values from -6 to 6
Outputs:
- layer_out: bfloat16 [32, 1024, 512], P('seq', 'blk')
- input_grad: bfloat16 [32, 1024, 512], P('seq', 'blk')
- grad_first_gain: float32 [512], replicated
- grad_first_shift: float32 [512], replicated
- grad_query_weight: float32 [512, 512], replicated
- grad_key_weight: float32 [512, 512], replicated
- grad_value_weight: float32 [512, 512], replicated
- grad_out_weight: float32 [512, 512], replicated
- grad_head_slopes: float32 [8], replicated
- grad_second_gain: float32 [512], replicated
- grad_second_shift: float32 [512], replicated
- grad_hidden_weight: float32 [512, 2048], replicated
- grad_output_weight: float32 [2048, 512], replicated
Inputs may be any that keep to these rules, and one draw needn't show every extreme that they name: `segment_ends`: each row rises strictly by 1 to 8 bytes from slot to slot; the first slot ends 1 to 8 bytes after the row's last memory end. In some sequence every step is 8 bytes; in another the first slot ends 1 byte after its memory. `memory_ends`: each row rises strictly by 1 to 8 bytes from entry to entry and its last entry is 0; in some sequence every step is 8 bytes. `segment_counts`: slots 0 to count - 1 of a sequence hold segments, the others are empty; some sequence uses all 1024 slots and some exactly half of them. `memory_lengths`: the last length memory rows of a sequence are valid; some sequence has all 512 and some a quarter.
All inputs are finite; a program needn't handle non-finite values.
Results may differ from a plain program's by a relative error of at most 0.022.
Values may be sent and summed in bfloat16 or wider, within the bound.
A program may use at most 256 MiB of HBM per device.

v0:
```python
import functools
import math

import jax
import jax.numpy as jnp
from jax import lax
from jax.experimental import pallas as pl
from jax.experimental.pallas import tpu as pltpu
from jax.sharding import PartitionSpec as P

epsilon = 1e-05
far_order = 1073741824
f32 = jnp.float32
bf16 = jnp.bfloat16
BLOCK = 256
LOG2E = 1.4426950408889634
LN2 = 0.6931471805599453


def dot_nn(left, right):
    return lax.dot_general(left, right, (((1,), (0,)), ((), ())), preferred_element_type=f32)


def dot_nt(left, right):
    return lax.dot_general(left, right, (((1,), (1,)), ((), ())), preferred_element_type=f32)


def norm_stats(values):
    centred = values - jnp.mean(values, axis=-1, keepdims=True)
    spread = jnp.mean(centred * centred, axis=-1, keepdims=True)
    scale = lax.rsqrt(spread + epsilon)
    return centred * scale, scale


def norm_back(unit, scale, grad_unit):
    mean_grad = jnp.mean(grad_unit, axis=-1, keepdims=True)
    mean_prod = jnp.mean(grad_unit * unit, axis=-1, keepdims=True)
    return (grad_unit - mean_grad - unit * mean_prod) * scale


def pieces_of(value, count):
    out = []
    for _ in range(count):
        part = value.astype(bf16).astype(f32)
        out.append(part)
        value = value - part
    return out


ERFC_P = 0.4
ERFC_C = (0.22567586600780487, 0.2256695181131363, 0.2078438550233841, 0.16853390634059906, 0.1414608359336853, -0.005667657125741243, 0.16915477812290192, -0.18294358253479004, 0.050272583961486816)


def gelu_both(x):
    cdf = 0.5 * lax.erf(x * math.sqrt(0.5)) + 0.5
    ex = jnp.exp2((x * x) * (-0.5 * LOG2E))
    return x * cdf, cdf + x * (ex * (1.0 / math.sqrt(2.0 * math.pi)))


def col_sum8(value):
    return jnp.sum(value.reshape(-1, 8, value.shape[-1]), axis=0)


def flip(bit):
    return 1 - bit


def layer_kernel(
    talk,
    counts_ref,
    lengths_ref,
    slopes_ref,
    tokens_ref,
    memory_ref,
    ends_ref,
    grad_ref,
    gain1_ref,
    shift1_ref,
    gain2_ref,
    shift2_ref,
    wq_hbm,
    wk_hbm,
    wv_hbm,
    wo_hbm,
    w1_hbm,
    w2_hbm,
    layer_hbm,
    ingrad_hbm,
    grads_hbm,
    small_ref,
    x_ref,
    mem_ref,
    og_ref,
    ends_s,
    wq_ref,
    wk_ref,
    wv_ref,
    wo_ref,
    w1_ref,
    w2_ref,
    keyint,
    k_s,
    v_s,
    kx,
    q_s,
    qt,
    rl_s,
    o_s,
    mixed,
    second_s,
    secondt,
    ogt,
    act_s,
    dpre_s,
    acc_s,
    dres,
    dolt,
    delta_s,
    g_s,
    rc_s,
    r1_s,
    sm_own,
    sm_in,
    load_sem,
    ex_send,
    ex_recv,
    ar_send,
    ar_recv,
    sm_send,
    sm_recv,
    out_sem,
    *probs,
):
    S, D = x_ref.shape
    M = mem_ref.shape[0]
    R = M + S
    FF = w1_ref.shape[1]
    H = slopes_ref.shape[0]
    DH = D // H
    HP = H // 2
    NB = S // BLOCK
    MB = M // BLOCK
    SH = S // 2
    MH = M // 2
    KC = 512
    CH = 512
    NC = FF // CH

    if talk:
        seq = lax.axis_index("seq")
        blk = lax.axis_index("blk")
    else:
        seq = 0
        blk = 0
    core = seq % 2
    why = (seq // 2) % 2
    zed = seq // 4

    def at(z=None, y=None, c=None, x=None):
        z = zed if z is None else z
        y = why if y is None else y
        c = core if c is None else c
        return {"seq": z * 4 + y * 2 + c, "blk": blk if x is None else x}

    sibling = at(c=flip(core))
    partner = at(x=flip(blk))
    z_to = [zed + 1 - 2 * (zed % 2), (zed + 2) % 4, 3 - zed]
    z_peers = [(at(z=z), z) for z in z_to]
    plane = blk * 2 + why
    xy_peers = [
        (at(y=flip(why)), blk * 2 + flip(why)),
        (at(x=flip(blk)), flip(blk) * 2 + why),
        (at(x=flip(blk), y=flip(why)), flip(blk) * 2 + flip(why)),
    ]

    def remote(src, dst, send, recv, device):
        return pltpu.make_async_remote_copy(
            src_ref=src,
            dst_ref=dst,
            send_sem=send,
            recv_sem=recv,
            device_id=device,
            device_id_type=pl.DeviceIdType.MESH,
        )

    other = 1 - blk

    def half_rows(half, size):
        return pl.ds(pl.multiple_of(half * size, BLOCK), size)

    def slot_piece(part, index, half, i):
        src = tokens_ref if part == 0 else grad_ref
        dst = x_ref if part == 0 else og_ref
        rows = pl.ds(pl.multiple_of(half * SH + i * BLOCK, BLOCK), BLOCK)
        return src.at[index, i * BLOCK : (i + 1) * BLOCK, :], dst.at[rows, :]

    nslot = SH // BLOCK
    loads = [
        (memory_ref.at[blk], mem_ref.at[half_rows(blk, MH), :]),
        (ends_ref.at[blk], ends_s.at[blk]),
        (wk_hbm, wk_ref),
        (wv_hbm, wv_ref),
        (wq_hbm, wq_ref),
    ]
    loads += [slot_piece(0, blk, blk, i) for i in range(nslot)]
    n_first = len(loads)
    loads += [(wo_hbm, wo_ref), (w1_hbm, w1_ref), (w2_hbm, w2_ref)]
    loads += [slot_piece(1, blk, blk, i) for i in range(nslot)]
    copies = [
        pltpu.make_async_copy(src, dst, load_sem.at[i]) for i, (src, dst) in enumerate(loads)
    ]
    sends = [
        (memory_ref.at[other], mem_ref.at[half_rows(blk, MH), :]),
        (ends_ref.at[other], ends_s.at[blk]),
    ]
    sends += [slot_piece(0, other, blk, i) for i in range(nslot)]
    sends += [slot_piece(1, other, blk, i) for i in range(nslot)]
    if talk:
        exchange = [
            remote(src, dst, ex_send.at[i], ex_recv.at[i], partner)
            for i, (src, dst) in enumerate(sends)
        ]
    else:
        local = [
            (memory_ref.at[other], mem_ref.at[half_rows(other, MH), :]),
            (ends_ref.at[other], ends_s.at[other]),
        ]
        local += [slot_piece(0, other, other, i) for i in range(nslot)]
        local += [slot_piece(1, other, other, i) for i in range(nslot)]
        exchange = [
            pltpu.make_async_copy(src, dst, ex_send.at[i]) for i, (src, dst) in enumerate(local)
        ]
    for copy in copies[:n_first]:
        copy.start()
    if talk:
        barrier = pltpu.get_barrier_semaphore()
        greet = [sibling] + [d for d, _ in z_peers] + [d for d, _ in xy_peers]
        for device in greet:
            pl.semaphore_signal(
                barrier, inc=1, device_id=device, device_id_type=pl.DeviceIdType.MESH
            )
        pl.semaphore_wait(barrier, len(greet))
    for copy in exchange:
        copy.start()
    for copy in copies[n_first:]:
        copy.start()

    def arrive(i):
        if talk:
            exchange[i].wait_recv()
        else:
            exchange[i].wait()

    directions = {
        "x": (blk, [(partner, other)]),
        "y": (why, [(at(y=flip(why)), flip(why))]),
        "a": (zed % 2, [(z_peers[0][0], 1 - zed % 2)]),
        "b": (zed // 2, [(z_peers[1][0], 1 - zed // 2)]),
        "z": (zed, z_peers),
        "p": (plane, xy_peers),
    }
    units = []
    for c in range(NC):
        width = 2 * CH // SPLIT[c]
        for i in range(SPLIT[c]):
            units.append((c * 2 * CH + i * width, width))
    units.append((2 * FF, D))
    for p in range(HP):
        units.append((2 * FF + D + p * 384, 384))
    HALF = D // 2

    def rows_at(start, size):
        return pl.ds(pl.multiple_of(start, 16), size)

    def unit_rounds(u):
        start, size, place = core * HALF, HALF, 0
        rounds = []
        for name in ORDERS[u]:
            mine, peers = directions[name]
            piece = size // (len(peers) + 1)
            rounds.append((start, piece, mine, peers, place))
            place += piece * len(peers)
            start, size = start + mine * piece, piece
        return rounds, start, size

    def unit_copies(u, step):
        col, width = units[u]
        cols = slice(col, col + width)
        rounds, start, size = unit_rounds(u)
        n = len(rounds)
        out = []
        if step == 0:
            rows = rows_at((1 - core) * HALF, HALF)
            out.append((g_s.at[rows, cols], rc_s.at[:, cols], sibling))
        elif step <= n:
            begin, piece, _, peers, place = rounds[step - 1]
            for d, (device, index) in enumerate(peers):
                rows = rows_at(begin + index * piece, piece)
                here = slice(place + d * piece, place + (d + 1) * piece)
                out.append((g_s.at[rows, cols], r1_s.at[here, cols], device))
        elif step <= 2 * n:
            level = 2 * n - step
            begin, piece, mine, peers, _ = rounds[level]
            rows = rows_at(begin + mine * piece, piece)
            src = g_s if level == n - 1 else grads_hbm
            for device, _ in peers:
                out.append((src.at[rows, cols], grads_hbm.at[rows, cols], device))
        else:
            rows = rows_at(core * HALF, HALF)
            out.append((grads_hbm.at[rows, cols], grads_hbm.at[rows, cols], sibling))
        first = 0
        for earlier in range(step):
            if 1 <= earlier <= n:
                first += len(rounds[earlier - 1][3])
            elif n < earlier <= 2 * n:
                first += len(rounds[2 * n - earlier][3])
            else:
                first += 1
        return [
            remote(src, dst, ar_send.at[u, first + k], ar_recv.at[u, first + k], device)
            for k, (src, dst, device) in enumerate(out)
        ]

    def unit_add(u, step):
        col, width = units[u]
        cols = slice(col, col + width)
        rounds, _, _ = unit_rounds(u)
        if step == 0:
            begin, piece, places, buffer = core * HALF, HALF, [0], rc_s
        else:
            begin, piece, mine, peers, place = rounds[step - 1]
            begin = begin + mine * piece
            places, buffer = [place + d * piece for d in range(len(peers))], r1_s
        block = min(piece, 64)

        def add(i, _):
            rows = rows_at(begin + i * block, block)
            total = g_s[rows, cols].astype(f32)
            for place in places:
                total = total + buffer[rows_at(place + i * block, block), cols].astype(f32)
            g_s[rows, cols] = total.astype(bf16)
            return 0

        if piece == block:
            add(0, 0)
        else:
            lax.fori_loop(0, piece // block, add, 0)

    def unit_out(u):
        col, width = units[u]
        cols = slice(col, col + width)
        _, start, size = unit_rounds(u)
        rows = rows_at(start, size) if talk else slice(0, D)
        return pltpu.make_async_copy(g_s.at[rows, cols], grads_hbm.at[rows, cols], out_sem.at[u])

    def advance(u, step):
        if not talk:
            return
        n = len(ORDERS[u])
        if step > 0:
            for copy in unit_copies(u, step - 1):
                copy.wait()
            if step - 1 <= n:
                unit_add(u, step - 1)
        if step == n + 1:
            unit_out(u).start()
        if step == n + 2:
            unit_out(u).wait()
        if step < 2 * n + 2:
            for copy in unit_copies(u, step):
                copy.start()

    def ticks(kind, index):
        moves = SCHEDULE.get((kind, index), ())
        if not moves:
            return

        @pl.when(seq >= 0)
        def _():
            for u, step in moves:
                if u < 0:
                    layer_copies[1 + step].start()
                else:
                    advance(u, step)

    def ticks_in_loop(kind, index, count, base=0):
        for k in range(count):
            if (kind, base + k) in SCHEDULE:

                @pl.when(index == k)
                def _():
                    ticks(kind, base + k)

    gain1 = gain1_ref[...]
    shift1 = shift1_ref[...]
    gain2 = gain2_ref[...]
    shift2 = shift2_ref[...]
    count = counts_ref[blk]
    length = lengths_ref[blk]

    def give(result, hbm, k, pieces):
        own = pltpu.make_async_copy(result.at[half_rows(blk, SH), :], hbm.at[blk], load_sem.at[k])
        moves = [own]
        size = SH // pieces
        for i in range(pieces):
            theirs = result.at[pl.ds(pl.multiple_of(other * SH + i * size, size), size), :]
            rows = slice(i * size, (i + 1) * size)
            sem = len(sends) + 4 * k + i
            if talk:
                there = hbm.at[blk, rows, :]
                moves.append(remote(theirs, there, ex_send.at[sem], ex_recv.at[sem], partner))
            else:
                moves.append(
                    pltpu.make_async_copy(theirs, hbm.at[other, rows, :], ex_send.at[sem])
                )
        return moves

    layer_copies = give(second_s, layer_hbm, 0, 4)
    ingrad_copies = give(second_s, ingrad_hbm, 1, nslot)

    def project(normed, key_rows):
        keyint[:, key_rows] = normed.T
        k_s[key_rows, :] = dot_nn(normed, wk_ref[...]).astype(bf16)
        v_s[key_rows, :] = dot_nn(normed, wv_ref[...]).astype(bf16)

    def norm_mem(b):
        rows = pl.ds(pl.multiple_of(b * BLOCK, BLOCK), BLOCK)
        unit, _ = norm_stats(mem_ref[rows, :].astype(f32))
        project((unit * gain1 + shift1).astype(bf16), rows)

    def norm_slot(b):
        rows = pl.ds(pl.multiple_of(b * BLOCK, BLOCK), BLOCK)
        key_rows = pl.ds(pl.multiple_of(b * BLOCK + M, BLOCK), BLOCK)
        unit, _ = norm_stats(x_ref[rows, :].astype(f32))
        normed = (unit * gain1 + shift1).astype(bf16)
        project(normed, key_rows)
        query = (dot_nn(normed, wq_ref[...]) * (LOG2E / math.sqrt(DH))).astype(bf16)
        q_s[rows, :] = query
        qt[:, rows] = query.T

    for copy in copies[:n_first]:
        copy.wait()
    mh = MH // BLOCK
    for i in range(mh):
        norm_mem(blk * mh + i)
    for i in range(nslot):
        norm_slot(blk * nslot + i)
    arrive(0)
    for i in range(mh):
        norm_mem(other * mh + i)
    arrive(1)

    lane = lax.broadcasted_iota(jnp.int32, (128, 128), 1)
    row = lax.broadcasted_iota(jnp.int32, (128, 128), 0)

    def end_row(start, size):
        if start < M:
            half, off = start // MH, start % MH
        else:
            half, off = (start - M) // SH, MH + (start - M) % SH
        return ends_s[half, :, off : off + size].astype(f32)

    for r in range(R // 128):
        end_col = jnp.broadcast_to(end_row(r * 128, 128), (128, 128)).T
        high = jnp.floor(end_col * (1.0 / 256.0)) * 256.0
        index = row + r * 128
        if r * 128 < M:
            valid = index >= M - length
        else:
            valid = index - M < count
        bias = jnp.where(valid, 0.0, -1e30)
        extra = jnp.where(lane < 3, high, jnp.where(lane < 6, end_col - high, bias))
        extra = jnp.where(lane == 7, 1.0, jnp.where(lane > 7, 0.0, extra))
        kx[r * 128 : (r + 1) * 128, :] = extra.astype(bf16)

    for i in range(nslot):
        arrive(2 + i)
        norm_slot(other * nslot + i)

    lane_q = lax.broadcasted_iota(jnp.int32, (BLOCK, 128), 1)
    first_half = lane_q < DH
    lane_row = lax.broadcasted_iota(jnp.int32, (1, 128), 1)

    def key_chunks(b):
        end = M + (b + 1) * BLOCK
        return [(start, min(KC, end - start)) for start in range(0, end, KC)]

    def key_full(lanes, start, size):
        return jnp.concatenate(
            [k_s[start : start + size, lanes], kx[start : start + size, :]], axis=1
        )

    def value_full(lanes, start, size):
        return jnp.concatenate(
            [v_s[start : start + size, lanes], jnp.ones((size, 128), bf16)], axis=1
        )

    def query_extra(head):
        slope = jnp.full((1, 128), slopes_ref[head] * LOG2E, f32)
        s1, s2, s3 = pieces_of(slope, 3)
        where = jnp.where(lane_row >= 3, lane_row - 3, lane_row)
        out = jnp.where(where == 0, s1, jnp.where(where == 1, s2, s3))
        return jnp.where(lane_row < 6, out, jnp.where(lane_row == 6, 1.0, 0.0))

    rl_s[...] = jnp.zeros_like(rl_s)
    for b in range(NB):
        rows = slice(b * BLOCK, (b + 1) * BLOCK)
        e_ref = probs[b]

        def fwd_pair(p, _):
            lanes = pl.ds(pl.multiple_of(p * 128, 128), 128)
            q_pair = q_s[rows, lanes]
            outs = []
            for half in range(2):
                keep = first_half if half == 0 else jnp.logical_not(first_half)
                q_half = jnp.where(keep, q_pair, jnp.zeros_like(q_pair))
                extra = jnp.broadcast_to(query_extra(2 * p + half), (BLOCK, 128)).astype(bf16)
                q_full = jnp.concatenate([q_half, extra], axis=1)
                chunks = key_chunks(b)
                scores = [dot_nt(q_full, key_full(lanes, k0, kn)) for k0, kn in chunks]
                below = lax.broadcasted_iota(
                    jnp.int32, (BLOCK, BLOCK), 1
                ) <= lax.broadcasted_iota(jnp.int32, (BLOCK, BLOCK), 0)
                last = scores[-1]
                cut = last.shape[1] - BLOCK
                diag = jnp.where(below, last[:, cut:], -1e30)
                scores[-1] = jnp.concatenate([last[:, :cut], diag], axis=1) if cut else diag
                top = scores[-1][:, 0:128]
                for part in scores:
                    for k in range(0, part.shape[1], 128):
                        top = jnp.maximum(top, part[:, k : k + 128])
                top = jnp.max(top, axis=1, keepdims=True)
                both = jnp.zeros((BLOCK, 256), f32)
                for part, (k0, kn) in zip(scores, chunks):
                    e = jnp.exp2(part - top).astype(bf16)
                    e_ref[2 * p + half, :, k0 : k0 + kn] = e
                    both = both + dot_nn(e, value_full(lanes, k0, kn))
                outs.append((both[:, 0:128], 1.0 / both[:, 128:256]))
            rl = jnp.where(first_half, outs[0][1], outs[1][1])
            o = jnp.where(first_half, outs[0][0], outs[1][0]) * rl
            packed = jnp.where(lane_q == 2 * p, outs[0][1], rl_s[rows, :])
            rl_s[rows, :] = jnp.where(lane_q == 2 * p + 1, outs[1][1], packed)
            o_low = o.astype(bf16)
            o_s[rows, lanes] = (o - o_low.astype(f32)).astype(bf16)
            mixed[rows, lanes] = o_low
            return 0

        lax.fori_loop(0, HP, fwd_pair, 0, unroll=2)

    for copy in copies[n_first:]:
        copy.wait()
    for i in range(nslot):
        arrive(2 + nslot + i)

    def residual_of(rows):
        return x_ref[rows, :].astype(f32) + dot_nn(mixed[rows, :], wo_ref[...])

    def feed_prep(b, _):
        rows = slice(b * BLOCK, (b + 1) * BLOCK)
        residual = residual_of(rows)
        unit, _ = norm_stats(residual)
        second = (unit * gain2 + shift2).astype(bf16)
        second_s[rows, :] = second
        secondt[:, rows] = second.T
        ogt[:, rows] = og_ref[rows, :].T
        acc_s[rows, :] = residual
        dres[rows, :] = jnp.zeros((BLOCK, D), f32)
        return 0

    for b in range(NB):
        feed_prep(b, 0)
    def feed_chunk(c, _):
        cols = pl.ds(pl.multiple_of(c * CH, CH), CH)
        for b in range(NB):
            rows = slice(b * BLOCK, (b + 1) * BLOCK)
            hidden = dot_nn(second_s[rows, :], w1_ref[:, cols])
            d_act = dot_nt(og_ref[rows, :], w2_ref[cols, :])
            act, slope = gelu_both(hidden)
            act = act.astype(bf16)
            d_pre = (d_act * slope).astype(bf16)
            act_s[rows, :] = act
            dpre_s[rows, :] = d_pre
            acc_s[rows, :] += dot_nn(act, w2_ref[cols, :])
            dres[rows, :] += dot_nt(d_pre, w1_ref[:, cols])
            for k in range(NC):
                if ("feed", k * NB + b) in SCHEDULE:

                    @pl.when(c == k)
                    def _():
                        ticks("feed", k * NB + b)

        for r in range(D // BLOCK):
            rows = slice(r * BLOCK, (r + 1) * BLOCK)
            pre_cols = pl.ds(pl.multiple_of(c * 2 * CH, CH), CH)
            act_cols = pl.ds(pl.multiple_of(c * 2 * CH + CH, CH), CH)
            g_s[rows, pre_cols] = dot_nn(secondt[rows, :], dpre_s[...]).astype(bf16)
            g_s[rows, act_cols] = dot_nn(ogt[rows, :], act_s[...]).astype(bf16)
        ticks_in_loop("chunk", c, NC)
        return 0

    lax.fori_loop(0, NC, feed_chunk, 0)

    def feed_post(b, sums):
        rows = slice(b * BLOCK, (b + 1) * BLOCK)
        unit, scale = norm_stats(residual_of(rows))
        d_second = dres[rows, :]
        d_residual = og_ref[rows, :].astype(f32) + norm_back(unit, scale, d_second * gain2)
        dres[rows, :] = d_residual
        d_branch = d_residual.astype(bf16)
        act_s[rows, :] = d_branch
        secondt[:, rows] = mixed[rows, :].T
        d_mixed = dot_nt(d_branch, wo_ref[...]).astype(bf16).astype(f32)
        rl_b = rl_s[rows, :]
        rl_wide = []
        for p in range(HP):
            first = jnp.broadcast_to(rl_b[:, 2 * p : 2 * p + 1], (BLOCK, 128))
            second = jnp.broadcast_to(rl_b[:, 2 * p + 1 : 2 * p + 2], (BLOCK, 128))
            rl_wide.append(jnp.where(first_half, first, second))
        dol_b = (d_mixed * jnp.concatenate(rl_wide, axis=1)).astype(bf16)
        o = mixed[rows, :].astype(f32) + o_s[rows, :].astype(f32)
        prod = dol_b.astype(f32) * o
        mixed[rows, :] = dol_b
        dolt[:, rows] = dol_b.T
        packed = jnp.zeros((BLOCK, 128), f32)
        for head in range(H):
            part = prod[:, (head // 2) * 128 : (head // 2 + 1) * 128]
            keep = first_half if head % 2 == 0 else jnp.logical_not(first_half)
            delta = jnp.sum(jnp.where(keep, part, 0.0), axis=1, keepdims=True)
            for k, piece in enumerate(pieces_of(jnp.broadcast_to(-delta, (BLOCK, 128)), 3)):
                packed = jnp.where(lane_q == 4 * head + k, piece, packed)
        delta_s[rows, :] = packed.astype(bf16)
        ticks("post", b)
        return sums[0] + col_sum8(d_second * unit), sums[1] + col_sum8(d_second)

    def feed_out(b, _):
        rows = pl.ds(pl.multiple_of(b * BLOCK, BLOCK), BLOCK)
        second_s[rows, :] = acc_s[rows, :].astype(bf16)
        return 0

    lax.fori_loop(0, NB, feed_out, 0)
    layer_copies[0].start()
    zero8 = jnp.zeros((8, D), f32)
    gain2_sum, shift2_sum = (zero8, zero8)
    for b in range(NB):
        gain2_sum, shift2_sum = feed_post(b, (gain2_sum, shift2_sum))
    for r in range(D // BLOCK):
        rows = slice(r * BLOCK, (r + 1) * BLOCK)
        g_s[rows, 2 * FF : 2 * FF + D] = dot_nn(secondt[rows, :], act_s[...]).astype(bf16)

    ticks("go", 0)

    small_ref[...] = jnp.zeros_like(small_ref)
    NK = R // KC
    lane_w = (lane_q == 0) | (lane_q == 3)

    def seen(b, j):
        return dict(enumerate(key_chunks(b - 1))).get(j, (0, 0))[1] if b else 0

    def gather(start, old, size, value):
        rows = slice(start, start + DH)
        if old:
            acc_s[rows, 0:old] += value[:, 0:old]
        if old < size:
            acc_s[rows, old:size] = value[:, old:size]

    def bwd_pair(p, slope_sums):
        lanes = pl.ds(pl.multiple_of(p * 128, 128), 128)
        for b in range(NB):
            rows = slice(b * BLOCK, (b + 1) * BLOCK)
            e_ref = probs[b]
            end_b = jnp.broadcast_to(end_row(M + b * BLOCK, BLOCK), (128, BLOCK)).T
            weight = jnp.where(lane_w, 1.0, jnp.where(lane_q == 7, -end_b, 0.0))
            dol_pair = mixed[rows, lanes]
            outs = []
            for half in range(2):
                head = 2 * p + half
                keep = first_half if half == 0 else jnp.logical_not(first_half)
                d_half = jnp.where(keep, dol_pair, jnp.zeros_like(dol_pair))
                delta = delta_s[rows, :]
                delta = jnp.where(lane_q // 4 == head, delta, jnp.zeros_like(delta))
                d_full = jnp.concatenate([d_half, delta], axis=1)
                hrows = pl.ds(pl.multiple_of(head * DH, DH), DH)
                q_t = qt[hrows, rows]
                d_t = dolt[hrows, rows]
                dqx = jnp.zeros((BLOCK, 256), f32)
                for j, (k0, kn) in enumerate(key_chunks(b)):
                    e = e_ref[head, :, k0 : k0 + kn]
                    ds = (dot_nt(d_full, value_full(lanes, k0, kn)) * e.astype(f32)).astype(bf16)
                    dqx = dqx + dot_nn(ds, key_full(lanes, k0, kn))
                    at_k = j * 128 + half * DH
                    gather(at_k, seen(b, j), kn, dot_nn(q_t, ds))
                    at_v = (NK + j) * 128 + half * DH
                    gather(at_v, seen(b, j), kn, dot_nn(d_t, e))
                outs.append(dqx[:, 0:128])
                tail = jnp.sum(dqx[:, 128:256] * weight, axis=0, keepdims=True)
                here = lax.broadcasted_iota(jnp.int32, (8, 128), 0) == head
                slope_sums = slope_sums + jnp.where(here, tail, 0.0)
            dq = jnp.where(first_half, outs[0], outs[1]) * (1.0 / math.sqrt(DH))
            q_s[rows, lanes] = dq.astype(bf16)
            for k in range(HP):
                if ("bwd", k * NB + b) in SCHEDULE:

                    @pl.when(p == k)
                    def _():
                        ticks("bwd", k * NB + b)

        for j in range(NK):
            dk = (acc_s[j * 128 : (j + 1) * 128, :] * LN2).astype(bf16).T
            k_s[j * KC : (j + 1) * KC, lanes] = dk
            dv = acc_s[(NK + j) * 128 : (NK + j + 1) * 128, :].astype(bf16).T
            v_s[j * KC : (j + 1) * KC, lanes] = dv
        for r in range(D // BLOCK):
            rows = slice(r * BLOCK, (r + 1) * BLOCK)
            gq = dot_nn(keyint[rows, M:], q_s[:, lanes]).astype(bf16)
            pair = jnp.concatenate([k_s[:, lanes], v_s[:, lanes]], axis=1)
            gkv = dot_nn(keyint[rows, :], pair).astype(bf16)
            col = 2 * FF + D + p * 384
            g_s[rows, pl.ds(pl.multiple_of(col, 128), 128)] = gq
            g_s[rows, pl.ds(pl.multiple_of(col + 128, 128), 256)] = gkv
        ticks_in_loop("pair", p, HP)
        return slope_sums

    slope_sums = lax.fori_loop(0, HP, bwd_pair, jnp.zeros((8, 128), f32))

    def key_back(key_rows):
        return dot_nt(k_s[key_rows, :], wk_ref[...]) + dot_nt(v_s[key_rows, :], wv_ref[...])

    def mem_back(b, sums):
        rows = pl.ds(pl.multiple_of(b * BLOCK, BLOCK), BLOCK)
        unit, _ = norm_stats(mem_ref[rows, :].astype(f32))
        d_rows = key_back(rows)
        return sums[0] + col_sum8(d_rows * unit), sums[1] + col_sum8(d_rows)

    def slot_back(b, sums):
        rows = pl.ds(pl.multiple_of(b * BLOCK, BLOCK), BLOCK)
        key_rows = pl.ds(pl.multiple_of(b * BLOCK + M, BLOCK), BLOCK)
        unit, scale = norm_stats(x_ref[rows, :].astype(f32))
        d_rows = key_back(key_rows) + dot_nt(q_s[rows, :], wq_ref[...])
        grad = norm_back(unit, scale, d_rows * gain1) + dres[rows, :]
        second_s[rows, :] = grad.astype(bf16)
        return sums[0] + col_sum8(d_rows * unit), sums[1] + col_sum8(d_rows)

    layer_copies[0].wait()
    for copy in layer_copies[1:]:
        if talk:
            copy.wait_send()
        else:
            copy.wait()
    sums = (zero8, zero8)
    for i in range(nslot):
        sums = slot_back(other * nslot + i, sums)
        ingrad_copies[1 + i].start()
        ticks("tail", i)
    for i in range(MB):
        sums = mem_back(i, sums)
        ticks("tail", nslot + i)
    for i in range(nslot):
        sums = slot_back(blk * nslot + i, sums)
        ticks("tail", nslot + MB + i)
    ingrad_copies[0].start()
    gain1_sum, shift1_sum = sums
    sm_own[0] = jnp.zeros_like(sm_own[0])
    for k, part in enumerate((gain1_sum, shift1_sum, gain2_sum, shift2_sum)):
        sm_own[0, k : k + 1, :] = jnp.sum(part, axis=0, keepdims=True)
    total = jnp.broadcast_to(jnp.sum(slope_sums, axis=1, keepdims=True), (8, 128))
    sm_own[0, 4:5, 0:128] = jnp.sum(
        jnp.where(lax.broadcasted_iota(jnp.int32, (8, 128), 0)
                  == lax.broadcasted_iota(jnp.int32, (8, 128), 1), total, 0.0),
        axis=0, keepdims=True)

    if talk:
        k = 0
        for level, devices in enumerate(
            ([sibling], [d for d, _ in z_peers], [d for d, _ in xy_peers])
        ):
            hops = []
            for device in devices:
                hops.append(
                    remote(sm_own.at[level], sm_in.at[k], sm_send.at[k], sm_recv.at[k], device)
                )
                k += 1
            for hop in hops:
                hop.start()
            ticks("small", level)
            total = sm_own[level]
            for i, hop in enumerate(hops):
                hop.wait()
                total = total + sm_in[k - len(hops) + i]
            sm_own[level + 1] = total
        small_ref[...] = sm_own[3]
    else:
        for level in range(3):
            ticks("small", level)
        small_ref[...] = sm_own[0]
    for i in range(10):
        ticks("last", i)
    ingrad_copies[0].wait()
    if not talk:
        for u in range(len(units)):
            unit_out(u).start()
            unit_out(u).wait()
    if talk:
        for copy in exchange:
            copy.wait_send()
        for copy in layer_copies[1:]:
            copy.wait_recv()
    for copy in ingrad_copies[1:]:
        copy.wait()


SPLIT = (2, 2, 2, 2)
ORDERS = ('axyb', 'yzx', 'yxz', 'yzx', 'xyab', 'yzx', 'ayxb', 'ayxb', 'xyab', 'yxab', 'zp', 'pz', 'zp')
SCHEDULE = {
    ('chunk', 0): ((0, 0), (1, 0)),
    ('chunk', 1): ((0, 1), (3, 0), (2, 0)),
    ('feed', 9): ((1, 1),),
    ('chunk', 2): ((5, 0), (3, 1), (4, 0)),
    ('feed', 13): ((0, 2), (2, 1)),
    ('feed', 15): ((1, 2),),
    ('chunk', 3): ((6, 0), (5, 1), (7, 0)),
    ('post', 0): ((4, 1),),
    ('post', 1): ((0, 3), (3, 2)),
    ('go', 0): ((6, 1), (8, 0)),
    ('bwd', 0): ((1, 3), (7, 1), (2, 2)),
    ('bwd', 1): ((4, 2),),
    ('bwd', 2): ((0, 4), (5, 2), (3, 3), (8, 1)),
    ('bwd', 3): ((1, 4), (6, 2)),
    ('pair', 0): ((9, 0), (3, 4), (4, 3), (2, 3)),
    ('bwd', 4): ((-1, 0), (0, 5), (7, 2)),
    ('bwd', 5): ((1, 5), (6, 3), (8, 2)),
    ('bwd', 6): ((-1, 1), (9, 1), (5, 3), (3, 5), (4, 4)),
    ('bwd', 7): ((0, 6), (7, 3), (2, 4)),
    ('pair', 1): ((-1, 2), (6, 4), (8, 3), (10, 0)),
    ('bwd', 8): ((9, 2),),
    ('bwd', 9): ((-1, 3), (0, 7), (1, 6)),
    ('bwd', 10): ((5, 4), (3, 6), (7, 4), (10, 1)),
    ('bwd', 11): ((4, 5), (8, 4)),
    ('pair', 2): ((6, 5), (9, 3), (11, 0), (2, 5)),
    ('bwd', 12): ((1, 7), (7, 5)),
    ('bwd', 14): ((0, 8), (3, 7), (11, 1)),
    ('bwd', 15): ((1, 8), (9, 4), (5, 5), (4, 6), (10, 2)),
    ('pair', 3): ((6, 6), (12, 0), (3, 8), (7, 6), (8, 5), (2, 6)),
    ('tail', 1): ((0, 9), (6, 7), (9, 5), (12, 1), (11, 2), (10, 3)),
    ('tail', 2): ((5, 6), (4, 7), (7, 7)),
    ('tail', 3): ((0, 10), (8, 6), (2, 7)),
    ('tail', 4): ((6, 8), (9, 6)),
    ('tail', 5): ((2, 8),),
    ('small', 0): ((5, 7), (12, 2), (4, 8), (8, 7), (11, 3)),
    ('small', 1): ((6, 9), (9, 7), (7, 8)),
    ('small', 2): ((5, 8), (12, 3), (8, 8), (11, 4), (10, 4)),
    ('last', 0): ((6, 10), (9, 8), (12, 4), (4, 9), (7, 9), (8, 9), (11, 5), (10, 5)),
    ('last', 1): ((9, 9), (12, 5), (4, 10), (7, 10), (8, 10), (11, 6), (10, 6)),
    ('last', 2): ((9, 10), (12, 6)),
}


def layer_call(counts, lengths, tokens, memory, ends, grad, params, talk=True):
    _, SH, D = tokens.shape
    MH = memory.shape[1]
    S, M = 2 * SH, 2 * MH
    R = M + S
    gain1, shift1, wq, wk, wv, wo, slopes, gain2, shift2, w1, w2 = params
    FF = w1.shape[1]
    H = slopes.shape[0]
    vmem = pl.BlockSpec(memory_space=pltpu.VMEM)
    smem = pl.BlockSpec(memory_space=pltpu.SMEM)
    hbm = pl.BlockSpec(memory_space=pl.ANY)
    V = pltpu.VMEM
    G = 2 * FF + 4 * D
    units = len(ORDERS)
    dma = pltpu.SemaphoreType.DMA
    scratch = [
        V((S, D), bf16),
        V((M, D), bf16),
        V((S, D), bf16),
        V((2, 1, MH + SH), jnp.int32),
        V((D, D), bf16),
        V((D, D), bf16),
        V((D, D), bf16),
        V((D, D), bf16),
        V((D, FF), bf16),
        V((FF, D), bf16),
        V((D, R), bf16),
        V((R, D), bf16),
        V((R, D), bf16),
        V((R, 128), bf16),
        V((S, D), bf16),
        V((D, S), bf16),
        V((S, 128), f32),
        V((S, D), bf16),
        V((S, D), bf16),
        V((S, D), bf16),
        V((D, S), bf16),
        V((D, S), bf16),
        V((S, 512), bf16),
        V((S, 512), bf16),
        V((S, D), f32),
        V((S, D), f32),
        V((D, S), bf16),
        V((S, 128), bf16),
        V((D, G), bf16),
        V((D // 2, G), bf16),
        V((D // 2 - 16, G), bf16),
        V((4, 8, D), f32),
        V((7, 8, D), f32),
        dma((16,)),
        dma((12,)),
        dma((12,)),
        dma((units, 14)),
        dma((units, 14)),
        dma((7,)),
        dma((7,)),
        dma((units,)),
    ]
    for b in range(S // BLOCK):
        scratch.append(V((H, BLOCK, M + (b + 1) * BLOCK), bf16))
    shapes = (
        jax.ShapeDtypeStruct((2, SH, D), bf16),
        jax.ShapeDtypeStruct((2, SH, D), bf16),
        jax.ShapeDtypeStruct((D, G), bf16),
        jax.ShapeDtypeStruct((8, D), f32),
    )
    extra = {"collective_id": 1, "has_side_effects": True} if talk else {}
    return pl.pallas_call(
        functools.partial(layer_kernel, talk),
        out_shape=shapes,
        in_specs=[smem] * 3 + [hbm] * 4 + [vmem] * 4 + [hbm] * 6,
        out_specs=[hbm, hbm, hbm, vmem],
        scratch_shapes=scratch,
        compiler_params=pltpu.CompilerParams(
            vmem_limit_bytes=64 * 1024 * 1024 - 65536, **extra
        ),
        name="layer",
    )(
        counts, lengths, slopes, tokens, memory, ends, grad,
        gain1.reshape(1, D), shift1.reshape(1, D), gain2.reshape(1, D), shift2.reshape(1, D),
        wq, wk, wv, wo, w1, w2,
    )


def layer_norm(values, gain, shift):
    centred = values - jnp.mean(values, axis=-1, keepdims=True)
    spread = jnp.mean(centred * centred, axis=-1, keepdims=True)
    return centred * lax.rsqrt(spread + epsilon) * gain + shift


def block_scores(
    q_heads, key_block, q_ends, key_order, key_ends, q_index, head_slopes, score_scale
):
    scores = (
        jnp.einsum("qhd,khd->hqk", q_heads, key_block, preferred_element_type=jnp.float32)
        * score_scale
    )
    distance = (q_ends[:, None] - key_ends[None, :]).astype(jnp.float32)
    scores = scores - head_slopes[:, None, None] * distance[None]
    allowed = key_order[None, :] <= q_index[:, None]
    return (jnp.where(allowed[None], scores, -1e30), distance)


def spread_device(
    tokens,
    memory,
    segment_ends,
    memory_ends,
    segment_counts,
    memory_lengths,
    first_gain,
    first_shift,
    query_weight,
    key_weight,
    value_weight,
    out_weight,
    head_slopes,
    second_gain,
    second_shift,
    hidden_weight,
    output_weight,
    output_grad,
):
    seq_count, slot_count, model_width = tokens.shape
    mem_count = memory.shape[1]
    head_count = head_slopes.shape[0]
    head_dim = model_width // head_count
    score_scale = 1.0 / math.sqrt(head_dim)
    key_rows = mem_count + slot_count
    blocks = lax.axis_size("blk")
    my_block = lax.axis_index("blk")
    x_float = tokens.astype(jnp.float32)
    mem_float = memory.astype(jnp.float32)
    normed = layer_norm(x_float, first_gain, first_shift).astype(jnp.bfloat16)
    mem_normed = layer_norm(mem_float, first_gain, first_shift).astype(jnp.bfloat16)
    key_input = jnp.concatenate([mem_normed, normed], axis=1)
    query = jnp.einsum(
        "std,de->ste", normed, query_weight, preferred_element_type=jnp.float32
    ).astype(jnp.bfloat16)
    pair_weight = jnp.concatenate([key_weight, value_weight], axis=1)
    key_value = jnp.einsum(
        "srd,de->rse", key_input, pair_weight, preferred_element_type=jnp.float32
    ).astype(jnp.bfloat16)
    mem_index = my_block * mem_count + jnp.arange(mem_count, dtype=jnp.int32)
    slot_index = my_block * slot_count + jnp.arange(slot_count, dtype=jnp.int32)
    mem_order = jnp.where(
        mem_index[None, :] >= mem_count * blocks - memory_lengths[:, None], -1, far_order
    )
    slot_order = jnp.where(
        slot_index[None, :] < segment_counts[:, None], slot_index[None, :], far_order
    )
    key_meta = jnp.stack(
        [
            jnp.concatenate([mem_order, slot_order], axis=1),
            jnp.concatenate([memory_ends, segment_ends], axis=1),
        ]
    )
    all_pairs, all_meta = (
        lax.all_gather(key_value, "blk", axis=0, tiled=True),
        lax.all_gather(key_meta, "blk", axis=2, tiled=True),
    )
    query_heads = query.reshape(seq_count, slot_count, head_count, head_dim)

    def pick(seq_index):
        pair_rows = lax.dynamic_index_in_dim(all_pairs, seq_index, 1, keepdims=False)
        meta_rows = lax.dynamic_index_in_dim(all_meta, seq_index, 1, keepdims=False)
        key_heads = pair_rows[:, :model_width].reshape(-1, key_rows, head_count, head_dim)
        value_heads = pair_rows[:, model_width:].reshape(-1, key_rows, head_count, head_dim)
        return (
            key_heads,
            value_heads,
            meta_rows[0].reshape(-1, key_rows),
            meta_rows[1].reshape(-1, key_rows),
        )

    def attend(seq_index):
        key_heads, value_heads, key_order, key_ends = pick(seq_index)
        q_heads = lax.dynamic_index_in_dim(query_heads, seq_index, 0, keepdims=False)
        q_ends = lax.dynamic_index_in_dim(segment_ends, seq_index, 0, keepdims=False)

        def stats_step(running, pieces):
            scores = block_scores(
                q_heads,
                pieces[0],
                q_ends,
                pieces[1],
                pieces[2],
                slot_index,
                head_slopes,
                score_scale,
            )[0]
            running_max = jnp.maximum(running[0], jnp.max(scores, axis=-1))
            running_sum = running[1] * jnp.exp(running[0] - running_max) + jnp.sum(
                jnp.exp(scores - running_max[..., None]), axis=-1
            )
            return ((running_max, running_sum), None)

        start_max = jnp.full((head_count, slot_count), -jnp.inf, jnp.float32)
        (top_max, top_sum), _ = lax.scan(
            stats_step, (start_max, jnp.zeros_like(start_max)), (key_heads, key_order, key_ends)
        )
        log_total = top_max + jnp.log(top_sum)

        def out_step(summed, pieces):
            scores = block_scores(
                q_heads,
                pieces[0],
                q_ends,
                pieces[1],
                pieces[2],
                slot_index,
                head_slopes,
                score_scale,
            )[0]
            attn_probs = jnp.exp(scores - log_total[..., None]).astype(jnp.bfloat16)
            return (
                summed
                + jnp.einsum(
                    "hqk,khd->qhd", attn_probs, pieces[3], preferred_element_type=jnp.float32
                ),
                None,
            )

        start_out = jnp.zeros((slot_count, head_count, head_dim), jnp.float32)
        mixed_heads, _ = lax.scan(
            out_step, start_out, (key_heads, key_order, key_ends, value_heads)
        )
        return (mixed_heads, log_total)

    mixed_all, log_totals = lax.map(attend, jnp.arange(seq_count))
    mixed_low = mixed_all.reshape(seq_count, slot_count, model_width).astype(jnp.bfloat16)
    residual = x_float + jnp.einsum(
        "std,de->ste", mixed_low, out_weight, preferred_element_type=jnp.float32
    )
    second_low = layer_norm(residual, second_gain, second_shift).astype(jnp.bfloat16)
    hidden_pre = jnp.einsum(
        "std,df->stf", second_low, hidden_weight, preferred_element_type=jnp.float32
    )
    act_low = jax.nn.gelu(hidden_pre, approximate=False).astype(jnp.bfloat16)
    layer_out = (
        residual
        + jnp.einsum("stf,fd->std", act_low, output_weight, preferred_element_type=jnp.float32)
    ).astype(jnp.bfloat16)
    grad_output_w = jnp.einsum(
        "stf,std->fd", act_low, output_grad, preferred_element_type=jnp.float32
    )
    d_act = jnp.einsum(
        "std,fd->stf", output_grad, output_weight, preferred_element_type=jnp.float32
    )
    _, gelu_pull = jax.vjp(lambda inner: jax.nn.gelu(inner, approximate=False), hidden_pre)
    d_pre_low = gelu_pull(d_act)[0].astype(jnp.bfloat16)
    grad_hidden_w = jnp.einsum(
        "std,stf->df", second_low, d_pre_low, preferred_element_type=jnp.float32
    )
    d_second = jnp.einsum(
        "stf,df->std", d_pre_low, hidden_weight, preferred_element_type=jnp.float32
    )
    _, second_pull = jax.vjp(layer_norm, residual, second_gain, second_shift)
    d_resid_norm, grad_second_g, grad_second_b = second_pull(d_second)
    d_residual = d_resid_norm + output_grad.astype(jnp.float32)
    d_branch = d_residual.astype(jnp.bfloat16)
    grad_out_w = jnp.einsum("std,ste->de", mixed_low, d_branch, preferred_element_type=jnp.float32)
    d_mixed = jnp.einsum(
        "ste,de->std", d_branch, out_weight, preferred_element_type=jnp.float32
    ).astype(jnp.bfloat16)
    d_mixed_heads = d_mixed.reshape(seq_count, slot_count, head_count, head_dim)

    def query_side(seq_index):
        key_heads, value_heads, key_order, key_ends = pick(seq_index)
        q_heads = lax.dynamic_index_in_dim(query_heads, seq_index, 0, keepdims=False)
        q_ends = lax.dynamic_index_in_dim(segment_ends, seq_index, 0, keepdims=False)
        d_heads = lax.dynamic_index_in_dim(d_mixed_heads, seq_index, 0, keepdims=False)
        log_total = lax.dynamic_index_in_dim(log_totals, seq_index, 0, keepdims=False)

        def probs_of(key_block, order_block, ends_block, value_block):
            scores, distance = block_scores(
                q_heads,
                key_block,
                q_ends,
                order_block,
                ends_block,
                slot_index,
                head_slopes,
                score_scale,
            )
            attn_probs = jnp.exp(scores - log_total[..., None])
            d_probs = jnp.einsum(
                "qhd,khd->hqk", d_heads, value_block, preferred_element_type=jnp.float32
            )
            return (attn_probs, d_probs, distance)

        def delta_step(summed, pieces):
            attn_probs, d_probs, _ = probs_of(pieces[0], pieces[1], pieces[2], pieces[3])
            return (summed + jnp.sum(attn_probs * d_probs, axis=-1), None)

        delta_rows, _ = lax.scan(
            delta_step,
            jnp.zeros((head_count, slot_count), jnp.float32),
            (key_heads, key_order, key_ends, value_heads),
        )

        def grad_step(running, pieces):
            attn_probs, d_probs, distance = probs_of(pieces[0], pieces[1], pieces[2], pieces[3])
            d_scores = (attn_probs * (d_probs - delta_rows[..., None])).astype(jnp.bfloat16)
            d_query = running[0] + jnp.einsum(
                "hqk,khd->qhd", d_scores, pieces[0], preferred_element_type=jnp.float32
            )
            d_slopes = running[1] - jnp.sum(
                d_scores.astype(jnp.float32) * distance[None], axis=(1, 2)
            )
            return ((d_query, d_slopes), None)

        start_grads = (
            jnp.zeros((slot_count, head_count, head_dim), jnp.float32),
            jnp.zeros((head_count,), jnp.float32),
        )
        (d_query, d_slopes), _ = lax.scan(
            grad_step, start_grads, (key_heads, key_order, key_ends, value_heads)
        )
        return (d_query * score_scale, delta_rows, d_slopes)

    d_query_all, delta_all, slope_parts = lax.map(query_side, jnp.arange(seq_count))
    grad_slopes = jnp.sum(slope_parts, axis=0)
    d_query_low = d_query_all.reshape(seq_count, slot_count, model_width).astype(jnp.bfloat16)

    def pair_terms(
        pair_rows, order_block, ends_block, q_heads, q_ends, q_index, d_heads, log_total, delta_rows
    ):
        key_block = pair_rows[:, :model_width].reshape(key_rows, head_count, head_dim)
        value_block = pair_rows[:, model_width:].reshape(key_rows, head_count, head_dim)
        scores, _ = block_scores(
            q_heads, key_block, q_ends, order_block, ends_block, q_index, head_slopes, score_scale
        )
        attn_probs = jnp.exp(scores - log_total[..., None])
        d_probs = jnp.einsum(
            "qhd,khd->hqk", d_heads, value_block, preferred_element_type=jnp.float32
        )
        d_scores = (attn_probs * (d_probs - delta_rows[..., None])).astype(jnp.bfloat16)
        d_value = jnp.einsum(
            "hqk,qhd->khd",
            attn_probs.astype(jnp.bfloat16),
            d_heads,
            preferred_element_type=jnp.float32,
        )
        d_key = (
            jnp.einsum("hqk,qhd->khd", d_scores, q_heads, preferred_element_type=jnp.float32)
            * score_scale
        )
        return jnp.concatenate(
            [d_key.reshape(key_rows, model_width), d_value.reshape(key_rows, model_width)], axis=1
        )

    def one_block(block_index):
        offset = block_index * key_rows
        pair_block = lax.dynamic_slice_in_dim(all_pairs, offset, key_rows, 0)
        meta_block = lax.dynamic_slice_in_dim(all_meta, offset, key_rows, 2)
        return jax.vmap(pair_terms, in_axes=(1, 0, 0, 0, 0, None, 0, 0, 0), out_axes=1)(
            pair_block,
            meta_block[0],
            meta_block[1],
            query_heads,
            segment_ends,
            slot_index,
            d_mixed_heads,
            log_totals,
            delta_all,
        )

    pieces = lax.map(one_block, jnp.arange(lax.axis_size("blk") * key_rows // key_rows))
    pair_grads = lax.psum_scatter(
        pieces.reshape(lax.axis_size("blk") * key_rows, seq_count, 2 * model_width).astype(
            jnp.bfloat16
        ),
        "blk",
        scatter_dimension=0,
        tiled=True,
    )
    grad_pair_w = jnp.einsum(
        "srd,rse->de", key_input, pair_grads, preferred_element_type=jnp.float32
    )
    grad_key_w = grad_pair_w[:, :model_width]
    grad_value_w = grad_pair_w[:, model_width:]
    d_key_input = jnp.einsum(
        "rse,de->srd", pair_grads, pair_weight, preferred_element_type=jnp.float32
    )
    grad_query_w = jnp.einsum(
        "std,ste->de", normed, d_query_low, preferred_element_type=jnp.float32
    )
    d_normed = (
        jnp.einsum("ste,de->std", d_query_low, query_weight, preferred_element_type=jnp.float32)
        + d_key_input[:, mem_count:]
    )
    _, first_pull = jax.vjp(layer_norm, x_float, first_gain, first_shift)
    d_tokens, gain_slots, shift_slots = first_pull(d_normed)
    _, mem_pull = jax.vjp(
        lambda gain, shift: layer_norm(mem_float, gain, shift), first_gain, first_shift
    )
    gain_mem, shift_mem = mem_pull(d_key_input[:, :mem_count])
    input_grad = (d_tokens + d_residual).astype(jnp.bfloat16)
    grad_first_g = gain_slots + gain_mem
    grad_first_b = shift_slots + shift_mem
    summed = lax.psum(
        (
            grad_first_g,
            grad_first_b,
            grad_query_w,
            grad_key_w,
            grad_value_w,
            grad_out_w,
            grad_slopes,
            grad_second_g,
            grad_second_b,
            grad_hidden_w,
            grad_output_w,
        ),
        ("seq", "blk"),
    )
    return (
        layer_out,
        input_grad,
        summed[0],
        summed[1],
        summed[2],
        summed[3],
        summed[4],
        summed[5],
        summed[6],
        summed[7],
        summed[8],
        summed[9],
        summed[10],
    )


def widen_kernel(ga, gb, gc, layer_in, grad_in, small, *outs):
    gw1, gw2, go, gq, gk, gv, layer, grad, gain1, shift1, slopes, gain2, shift2 = outs
    half = ga.shape[1] // 2
    gw1[...] = ga[:, :half].astype(f32)
    gw2[...] = ga[:, half:].astype(f32).T
    go[...] = gb[...].astype(f32)
    for i, out in enumerate((gq, gk, gv)):
        out[...] = gc[:, i * 128 : (i + 1) * 128].astype(f32)
    layer[...] = layer_in[...]
    grad[...] = grad_in[...]

    @pl.when((pl.program_id(0) == 0) & (pl.program_id(1) == 0))
    def _():
        for i, out in enumerate((gain1, shift1, gain2, shift2)):
            out[...] = small[i : i + 1, :]
        slopes[...] = small[4:5, 0:8]


def widen(grads, layer, in_grad, small, D, FF):
    RB = D // 2
    LB = layer.shape[0] // 8
    out = [
        ((D, FF), (RB, 512), lambda c, r: (r, c)),
        ((FF, D), (512, RB), lambda c, r: (c, r)),
        ((D, D), (RB, 128), lambda c, r: (r, c)),
        ((D, D), (RB, 128), lambda c, r: (r, c)),
        ((D, D), (RB, 128), lambda c, r: (r, c)),
        ((D, D), (RB, 128), lambda c, r: (r, c)),
        ((8 * LB, D), (LB, D), lambda c, r: (2 * c + r, 0)),
        ((8 * LB, D), (LB, D), lambda c, r: (2 * c + r, 0)),
    ]
    kinds = [f32] * 6 + [bf16] * 2
    shapes = [jax.ShapeDtypeStruct(shape, kind) for (shape, _, _), kind in zip(out, kinds)]
    specs = [pl.BlockSpec(block, index) for _, block, index in out]
    for width in (D, D, 8, D, D):
        shapes.append(jax.ShapeDtypeStruct((1, width), f32))
        specs.append(pl.BlockSpec((1, width), lambda c, r: (0, 0)))
    go_at = 2 * FF // 128
    head_at = (2 * FF + D) // 384
    return pl.pallas_call(
        widen_kernel,
        grid=(4, 2),
        out_shape=shapes,
        in_specs=[
            pl.BlockSpec((RB, 1024), lambda c, r: (r, c)),
            pl.BlockSpec((RB, 128), lambda c, r: (r, go_at + c)),
            pl.BlockSpec((RB, 384), lambda c, r: (r, head_at + c)),
            pl.BlockSpec((LB, D), lambda c, r: (2 * c + r, 0)),
            pl.BlockSpec((LB, D), lambda c, r: (2 * c + r, 0)),
            pl.BlockSpec((8, D), lambda c, r: (0, 0)),
        ],
        out_specs=specs,
        compiler_params=pltpu.CompilerParams(vmem_limit_bytes=62 * 1024 * 1024),
        name="widen",
    )(grads, grads, grads, layer, in_grad, small)


def whole_device(*args):
    tokens, memory, segment_ends, memory_ends, counts, lengths = args[:6]
    params = args[6:17]
    output_grad = args[17]
    D = tokens.shape[2]
    FF = params[9].shape[1]
    H = params[6].shape[0]
    ends = jnp.concatenate([memory_ends, segment_ends], axis=1)[:, None]
    layer, in_grad, grads, small = layer_call(
        counts, lengths, tokens, memory, ends, output_grad, params
    )
    gw1, gw2, go, gq, gk, gv, layer, in_grad, *rows = widen(
        grads, layer.reshape(-1, D), in_grad.reshape(-1, D), small, D, FF
    )
    gain1, shift1, slopes, gain2, shift2 = (row[0] for row in rows)
    return (
        layer.reshape(tokens.shape),
        in_grad.reshape(tokens.shape),
        gain1,
        shift1,
        gq,
        gk,
        gv,
        go,
        slopes,
        gain2,
        shift2,
        gw1,
        gw2,
    )


def per_device(*args):
    whole = args[0].shape[0] == lax.axis_size("blk") == 2 and lax.axis_size("seq") == 16
    if whole:
        return whole_device(*args)
    return spread_device(*args)


def solution(mesh):
    placed = (
        P("seq", "blk", None),
        P("seq", "blk", None),
        P("seq", "blk"),
        P("seq", "blk"),
        P("seq"),
        P("seq"),
        P(),
        P(),
        P(),
        P(),
        P(),
        P(),
        P(),
        P(),
        P(),
        P(),
        P(),
        P("seq", "blk", None),
    )
    return jax.shard_map(
        per_device,
        mesh=mesh,
        in_specs=placed,
        out_specs=(
            P("seq", "blk", None),
            P("seq", "blk", None),
            P(),
            P(),
            P(),
            P(),
            P(),
            P(),
            P(),
            P(),
            P(),
            P(),
            P(),
        ),
        check_vma=False,
    )
```

profile of v0, /device:TPU:0, one launch (start us, length us, event | category | flops | bytes accessed | tf_op | source)
XLA Modules:
  0.0 153.9 jit_solution(13432995980194536121)
XLA Ops:
  0.6 0.7 pad_add_fusion
  1.3 0.6 broadcast_in_dim.3.ends_ref
  1.9 141.1 %layer.1 = (bf16[2,512,512]{2,1,0:T(8,128)(2,1)}, bf16[2,512,512]{2,1,0:T(8,128)(2,1)}, bf16[512,6144]{1,0:T(8,128)(2,1)}, f32[8,512]{1,0:T(8,128)}) custom-call(s32[2]{0:T(128)} %counts_ref.1, s32[2]{0:T(128)} %lengths_ref.1, f32[8]{0:T(128)} %slopes_ref.1, bf16[2,512,512]{2,1,0:T(8,128)(2,1)} %tokens_ref.1, bf16[2,256,512]{2,1,0:T(8,128)(2,1)} %memory_ref.1, ...), custom_call_target="tpu_custom_call" | custom-call | tf_op jit(solution)/shard_map/layer/pallas_call | solution.py:924
  143.1 10.6 %widen.1 = (f32[512,2048]{1,0:T(8,128)}, f32[2048,512]{1,0:T(8,128)}, f32[512,512]{1,0:T(8,128)}, f32[512,512]{1,0:T(8,128)}, f32[512,512]{1,0:T(8,128)}, /*inde...) custom-call(bf16[512,6144]{1,0:T(8,128)(2,1)} %get-tuple-element.30., ...), custom_call_target="tpu_custom_call" | custom-call | tf_op jit(solution)/shard_map/widen/pallas_call | solution.py:1330
where the time goes:
time: 154 us
  Pallas kernels  152 us (99%)
    pallas_call x1, Pallas kernels, layer_call(): pl.pallas_call(functools.partial(layer_kernel, talk), out_shape=shapes, i...  141 us
    pallas_call x1, Pallas kernels, widen(): pl.pallas_call(widen_kernel, grid=(4, 2), out_shape=shapes, in_specs=[pl....  10.6 us

commit v1 on v0

--- a/solution.py
+++ b/solution.py
@@ -1307,8 +1307,8 @@
 
 
 def widen(grads, layer, in_grad, small, D, FF):
-    RB = D // 2
-    LB = layer.shape[0] // 8
+    RB = D
+    LB = layer.shape[0] // 4
     out = [
         ((D, FF), (RB, 512), lambda c, r: (r, c)),
         ((FF, D), (512, RB), lambda c, r: (c, r)),
@@ -1316,8 +1316,8 @@
         ((D, D), (RB, 128), lambda c, r: (r, c)),
         ((D, D), (RB, 128), lambda c, r: (r, c)),
         ((D, D), (RB, 128), lambda c, r: (r, c)),
-        ((8 * LB, D), (LB, D), lambda c, r: (2 * c + r, 0)),
-        ((8 * LB, D), (LB, D), lambda c, r: (2 * c + r, 0)),
+        ((4 * LB, D), (LB, D), lambda c, r: (c, 0)),
+        ((4 * LB, D), (LB, D), lambda c, r: (c, 0)),
     ]
     kinds = [f32] * 6 + [bf16] * 2
     shapes = [jax.ShapeDtypeStruct(shape, kind) for (shape, _, _), kind in zip(out, kinds)]
@@ -1329,14 +1329,14 @@
     head_at = (2 * FF + D) // 384
     return pl.pallas_call(
         widen_kernel,
-        grid=(4, 2),
+        grid=(4, 1),
         out_shape=shapes,
         in_specs=[
             pl.BlockSpec((RB, 1024), lambda c, r: (r, c)),
             pl.BlockSpec((RB, 128), lambda c, r: (r, go_at + c)),
             pl.BlockSpec((RB, 384), lambda c, r: (r, head_at + c)),
-            pl.BlockSpec((LB, D), lambda c, r: (2 * c + r, 0)),
-            pl.BlockSpec((LB, D), lambda c, r: (2 * c + r, 0)),
+            pl.BlockSpec((LB, D), lambda c, r: (c, 0)),
+            pl.BlockSpec((LB, D), lambda c, r: (c, 0)),
             pl.BlockSpec((8, D), lambda c, r: (0, 0)),
         ],
         out_specs=specs,

time: 154 us -> 153 us (level)
  no operation moved by 1% of the time
where the time goes in v1:
time: 153 us
  Pallas kernels  151 us (99%)
    pallas_call x1, Pallas kernels, layer_call(): pl.pallas_call(functools.partial(layer_kernel, talk), out_shape=shapes, i...  141 us
    pallas_call x1, Pallas kernels, widen(): pl.pallas_call(widen_kernel, grid=(4, 1), out_shape=shapes, in_specs=[pl....  9.68 us

profile of v1, /device:TPU:0, one launch (start us, length us, event | category | flops | bytes accessed | tf_op | source)
XLA Modules:
  0.0 152.9 jit_solution(9387952302392541155)
XLA Ops:
  0.6 0.7 pad_add_fusion
  1.3 0.6 broadcast_in_dim.3.ends_ref
  1.9 141.1 %layer.1 = (bf16[2,512,512]{2,1,0:T(8,128)(2,1)}, bf16[2,512,512]{2,1,0:T(8,128)(2,1)}, bf16[512,6144]{1,0:T(8,128)(2,1)}, f32[8,512]{1,0:T(8,128)}) custom-call(s32[2]{0:T(128)} %counts_ref.1, s32[2]{0:T(128)} %lengths_ref.1, f32[8]{0:T(128)} %slopes_ref.1, bf16[2,512,512]{2,1,0:T(8,128)(2,1)} %tokens_ref.1, bf16[2,256,512]{2,1,0:T(8,128)(2,1)} %memory_ref.1, ...), custom_call_target="tpu_custom_call" | custom-call | tf_op jit(solution)/shard_map/layer/pallas_call | solution.py:924
  143.1 9.7 %widen.1 = (f32[512,2048]{1,0:T(8,128)}, f32[2048,512]{1,0:T(8,128)}, f32[512,512]{1,0:T(8,128)}, f32[512,512]{1,0:T(8,128)}, f32[512,512]{1,0:T(8,128)}, /*inde...) custom-call(bf16[512,6144]{1,0:T(8,128)(2,1)} %get-tuple-element.30., ...), custom_call_target="tpu_custom_call" | custom-call | tf_op jit(solution)/shard_map/widen/pallas_call | solution.py:1330
